TPU v7x, 512 devices: a whole 4x8x8 slice. The times are simulated.
512 devices in a mesh: rows: 64 (over y, x, core), rhs: 8 (over z).
Axes of the slice: x: 4, y: 8, z: 8, core: 2. Of those that a mesh axis runs over, the one named last changes fastest.
Arguments:
- right_side: float32 [64, 32768], P('rhs', 'rows'), may hold values from -6 to 6
- tiles: float32 [512, 7, 64, 64], P('rows'), may hold values from -2 to 5.5, as said below
- pivots: float32 [512, 64, 64], P('rows'), may hold values from -0.05 to 0.8, as said below
- columns: int32 [512, 7], P('rows'), may hold values from 0 to 511, as said below
Outputs:
- solution: float32 [64, 32768], P('rhs', 'rows')
- residual: float32 [64, 32768], P('rhs', 'rows')
Inputs may be any that keep to these rules, and one draw needn't show every extreme that they name: columns[i, 0] = i. The other six columns of block row i are i - o and i + o for three offsets o shared by all block rows, the largest of them exactly 8, in an order of the slots drawn for each block row; a column that would fall outside 0 to 511 is i itself. tiles[i, 0] is the diagonal tile of block row i; A is symmetric positive definite: the tile of block row i in a slot whose column j differs from i is the transpose of the tile of block row j in its slot whose column is i. Every pivots[i] is symmetric positive definite.
All inputs are finite; a program needn't handle non-finite values.
Results may differ from a plain program's by a relative error of at most 0.0003.
Values sent between devices are 32-bit elements; how exact they have to be, the bound alone decides.
A program may use at most 64 MiB of HBM per device.

v0:
```python
import jax
import jax.numpy as jnp
from jax import lax
from jax.sharding import PartitionSpec as P

SPAN = 8
ITERS = 2


def passed_along(value, axis, steps):
    count = lax.axis_size(axis)
    first, last = (max(0, -steps), min(count, count - steps))
    return lax.ppermute(value, axis, [(source, source + steps) for source in range(first, last)])


def extended_2(block, sides, width):
    for axis, dim in sides:
        count = lax.axis_size(axis)
        forward = [(i, i + 1) for i in range(count - 1)]
        backward = [(target, source) for source, target in forward]
        low = lax.ppermute(
            lax.slice_in_dim(block, block.shape[dim] - width, None, axis=dim), axis, forward
        )
        high = lax.ppermute(lax.slice_in_dim(block, 0, width, axis=dim), axis, backward)
        block = jnp.concatenate([low, block, high], axis=dim)
    return block


def inner(left, right):
    return jnp.dot(left, right.T, precision=lax.Precision.HIGHEST)


def chol_solve(factor, values):
    middle = lax.linalg.triangular_solve(factor, values, left_side=True, lower=True)
    return lax.linalg.triangular_solve(factor, middle, left_side=True, lower=True, transpose_a=True)


def shards(right_side, tiles, pivots, columns):
    count = right_side.shape[0]
    shard_rows = tiles.shape[0]
    width = tiles.shape[2]
    cells = shard_rows * width
    where_row = lax.axis_index("rows")
    start = where_row * shard_rows
    position = where_row % SPAN
    block_low = (where_row - position) * shard_rows
    block_high = block_low + SPAN * shard_rows
    global_rows = start + jnp.arange(shard_rows, dtype=jnp.int32)
    lower = (columns < global_rows[:, None]) & (columns >= block_low)
    upper = (columns > global_rows[:, None]) & (columns < block_high)
    lower_tiles = tiles * lower[:, :, None, None].astype(tiles.dtype)
    upper_tiles = tiles * upper[:, :, None, None].astype(tiles.dtype)
    forward_cols = jnp.clip(columns - start + shard_rows, 0, 2 * shard_rows - 1)
    backward_cols = jnp.clip(columns - start, 0, 2 * shard_rows - 1)
    halo_cols = columns - start + shard_rows
    from_below = (position != 0).astype(jnp.float32)
    from_above = (position != SPAN - 1).astype(jnp.float32)

    def forward_local(source, incoming):
        extended = jnp.concatenate([incoming, jnp.zeros_like(source)], axis=1)

        def forward_one_row(row, extended):
            picked = jnp.take(extended, forward_cols[row], axis=1)
            summed = jnp.einsum(
                "kab,ckb->ca", lower_tiles[row], picked, precision=lax.Precision.HIGHEST
            )
            remain = source[:, row] - summed
            value = jnp.einsum("ab,cb->ca", pivots[row], remain, precision=lax.Precision.HIGHEST)
            return lax.dynamic_update_slice_in_dim(extended, value[:, None], shard_rows + row, 1)

        extended = lax.fori_loop(0, shard_rows, forward_one_row, extended)
        return extended[:, shard_rows:]

    def backward_local(source, incoming):
        extended = jnp.concatenate([jnp.zeros_like(source), incoming], axis=1)

        def backward_one_row(turn, extended):
            row = shard_rows - 1 - turn
            picked = jnp.take(extended, backward_cols[row], axis=1)
            summed = jnp.einsum(
                "kab,ckb->ca", upper_tiles[row], picked, precision=lax.Precision.HIGHEST
            )
            value = source[:, row] - jnp.einsum(
                "ab,cb->ca", pivots[row], summed, precision=lax.Precision.HIGHEST
            )
            return lax.dynamic_update_slice_in_dim(extended, value[:, None], row, 1)

        extended = lax.fori_loop(0, shard_rows, backward_one_row, extended)
        return extended[:, :shard_rows]

    def precondition(vector):
        source = vector.reshape(count, shard_rows, width)
        lowered = forward_local(source, jnp.zeros_like(source))
        for turn in range(SPAN - 1):
            incoming = passed_along(lowered, "rows", 1) * from_below
            lowered = forward_local(source, incoming)
        result = backward_local(lowered, jnp.zeros_like(lowered))
        for turn in range(SPAN - 1):
            incoming = passed_along(result, "rows", -1) * from_above
            result = backward_local(lowered, incoming)
        return result.reshape(count, cells)

    solution = jnp.zeros_like(right_side)
    residual = right_side
    direction = precondition(residual)
    for turn in range(ITERS):
        blocks = extended_2(direction, (("rows", 1),), cells).reshape(count, 3 * shard_rows, width)
        apply_picked = jnp.take(blocks, halo_cols, axis=1)
        image = jnp.einsum(
            "ikab,cikb->cia", tiles, apply_picked, precision=lax.Precision.HIGHEST
        ).reshape(count, cells)
        every_direction = lax.all_gather(direction, "rhs", axis=0, tiled=True)
        partial_pq = inner(every_direction, image)
        partial_pr = inner(every_direction, residual)
        summed_pq, summed_pr = lax.psum((partial_pq, partial_pr), "rows")
        gram = lax.all_gather(summed_pq, "rhs", axis=1, tiled=True)
        factor = jnp.linalg.cholesky(0.5 * (gram + gram.T))
        alpha = chol_solve(factor, summed_pr)
        change = jnp.dot(alpha.T, every_direction, precision=lax.Precision.HIGHEST)
        solution = solution + change
        if turn + 1 < ITERS:
            every_image = lax.all_gather(image, "rhs", axis=0, tiled=True)
            residual = residual - jnp.dot(alpha.T, every_image, precision=lax.Precision.HIGHEST)
            preconditioned = precondition(residual)
            summed_qz = lax.psum(inner(every_image, preconditioned), "rows")
            beta = -chol_solve(factor, summed_qz)
            direction = preconditioned + jnp.dot(
                beta.T, every_direction, precision=lax.Precision.HIGHEST
            )
        else:
            every_image = lax.all_gather(image, "rhs", axis=0, tiled=True)
            residual = residual - jnp.dot(alpha.T, every_image, precision=lax.Precision.HIGHEST)
    return (solution, residual)


def solution(mesh):
    return jax.shard_map(
        shards,
        mesh=mesh,
        in_specs=(
            P("rhs", "rows"),
            P("rows", None, None, None),
            P("rows", None, None),
            P("rows", None),
        ),
        out_specs=(P("rhs", "rows"), P("rhs", "rows")),
        check_vma=False,
    )
```

profile of v0, /device:TPU:32, one launch (start us, length us, event | category | flops | bytes accessed | tf_op | source)
XLA Modules:
  0.0 1239.9 jit_solution(11222102633937518841)
XLA Ops:
  6.0 16.7 %while.480 = (s32[]{:T(128)}, f32[8,16,64]{2,0,1:T(8,128)S(1)}, f32[8,8,64]{2,0,1:T(8,128)S(1)}, s32[8,7]{1,0:T(8,128)S(1)}, f32[8,7,64,64]{3,2,1,0:T(8,128)}, /...) while((s32[]{:T(128)}, f32[8,16,64]{2,0,1:T(8,128)S(1)}, ...), condition=%wide.region_1.3_spmd, body=%wide.region_0.2_spmd.sunk | while | flops 3150896 | bytes 322845 | solution.py:71
  31.3 16.7 %while.481 = (s32[]{:T(128)}, f32[8,16,64]{2,0,1:T(8,128)S(1)}, f32[8,8,64]{2,0,1:T(8,128)S(1)}, s32[8,7]{1,0:T(8,128)S(1)}, f32[8,7,64,64]{3,2,1,0:T(8,128)}, /...) while((s32[]{:T(128)}, f32[8,16,64]{2,0,1:T(8,128)S(1)}, ...), condition=%wide.region_3.5_spmd, body=%wide.region_2.4_spmd.sunk | while | flops 3150896 | bytes 322845 | solution.py:71
  50.0 6.6 collective-permute-done.1
  56.6 16.7 %while.482 = (s32[]{:T(128)}, f32[8,16,64]{2,0,1:T(8,128)S(1)}, f32[8,8,64]{2,0,1:T(8,128)S(1)}, s32[8,7]{1,0:T(8,128)S(1)}, f32[8,7,64,64]{3,2,1,0:T(8,128)}, /...) while((s32[]{:T(128)}, f32[8,16,64]{2,0,1:T(8,128)S(1)}, ...), condition=%wide.region_5.7_spmd, body=%wide.region_4.6_spmd.sunk | while | flops 3150896 | bytes 322845 | solution.py:71
  75.3 6.6 collective-permute-done.2
  81.9 16.7 %while.483 = (s32[]{:T(128)}, f32[8,16,64]{2,0,1:T(8,128)S(1)}, f32[8,8,64]{2,0,1:T(8,128)S(1)}, s32[8,7]{1,0:T(8,128)S(1)}, f32[8,7,64,64]{3,2,1,0:T(8,128)}, /...) while((s32[]{:T(128)}, f32[8,16,64]{2,0,1:T(8,128)S(1)}, ...), condition=%wide.region_7.9_spmd, body=%wide.region_6.8_spmd.sunk | while | flops 3150896 | bytes 322845 | solution.py:71
  100.6 6.6 collective-permute-done.3
  107.2 16.7 %while.484 = (s32[]{:T(128)}, f32[8,16,64]{2,0,1:T(8,128)S(1)}, f32[8,8,64]{2,0,1:T(8,128)S(1)}, s32[8,7]{1,0:T(8,128)S(1)}, f32[8,7,64,64]{3,2,1,0:T(8,128)}, /...) while((s32[]{:T(128)}, f32[8,16,64]{2,0,1:T(8,128)S(1)}, ...), condition=%wide.region_9.11_spmd, body=%wide.region_8.10_spmd.sunk | while | flops 3150896 | bytes 322845 | solution.py:71
  125.9 6.6 collective-permute-done.4
  132.5 16.7 %while.485 = (s32[]{:T(128)}, f32[8,16,64]{2,0,1:T(8,128)S(1)}, f32[8,8,64]{2,0,1:T(8,128)S(1)}, s32[8,7]{1,0:T(8,128)S(1)}, f32[8,7,64,64]{3,2,1,0:T(8,128)}, /...) while((s32[]{:T(128)}, f32[8,16,64]{2,0,1:T(8,128)S(1)}, ...), condition=%wide.region_11.13_spmd, body=%wide.region_10.12_spmd.sunk | while | flops 3150896 | bytes 322845 | solution.py:71
  151.2 6.6 collective-permute-done.5
  157.8 16.7 %while.486 = (s32[]{:T(128)}, f32[8,16,64]{2,0,1:T(8,128)S(1)}, f32[8,8,64]{2,0,1:T(8,128)S(1)}, s32[8,7]{1,0:T(8,128)S(1)}, f32[8,7,64,64]{3,2,1,0:T(8,128)}, /...) while((s32[]{:T(128)}, f32[8,16,64]{2,0,1:T(8,128)S(1)}, ...), condition=%wide.region_13.15_spmd, body=%wide.region_12.14_spmd.sunk | while | flops 3150896 | bytes 322845 | solution.py:71
  176.5 6.6 collective-permute-done.6
  183.1 16.7 %while.487 = (s32[]{:T(128)}, f32[8,16,64]{2,0,1:T(8,128)S(1)}, f32[8,8,64]{2,0,1:T(8,128)S(1)}, s32[8,7]{1,0:T(8,128)S(1)}, f32[8,7,64,64]{3,2,1,0:T(8,128)}, /...) while((s32[]{:T(128)}, f32[8,16,64]{2,0,1:T(8,128)S(1)}, ...), condition=%wide.region_15.17_spmd, body=%wide.region_14.16_spmd.sunk | while | flops 3150896 | bytes 322845 | solution.py:71
  199.9 9.2 while.488
  212.6 9.2 while.489
  221.8 7.0 collective-permute-start.8
  230.4 9.2 while.490
  239.6 7.0 collective-permute-start.9
  248.2 9.2 while.491
  257.4 7.0 collective-permute-start.10
  266.0 9.2 while.492
  275.2 7.0 collective-permute-start.11
  283.8 9.2 while.493
  293.0 7.0 collective-permute-start.12
  301.6 9.2 while.494
  310.8 7.0 collective-permute-start.13
  319.4 9.2 while.495
  330.6 7.0 collective-permute-start.15
  337.6 30.9 %all_gather.18 = f32[64,512]{1,0:T(8,128)S(1)} all-gather(f32[8,512]{1,0:T(8,128)S(1)} %reshape.66), channel_id=1, replica_groups=mesh['rows'=64,'rhs'=8] {'rhs'}, dimensions={0}, use_global_device_ids=true | all-gather | bytes 147456 | tf_op jit(solution)/shard_map/all_gather | solution.py:112
  373.2 24.6 %all_gather.20 = f32[64,512]{1,0:T(8,128)S(1)} all-gather(f32[8,512]{1,0:T(8,128)S(1)} %reshape.67), channel_id=1, replica_groups=mesh['rows'=64,'rhs'=8] {'rhs'}, dimensions={0}, use_global_device_ids=true | all-gather | bytes 147456 | tf_op jit(solution)/shard_map/all_gather | solution.py:122
  397.8 126.1 %all-reduce.29 = (f32[64,8]{0,1:T(8,128)S(1)}, f32[64,8]{0,1:T(8,128)S(1)}) all-reduce(f32[64,8]{0,1:T(8,128)S(1)} %fusion.476, f32[64,8]{0,1:T(8,128)S(1)} %fusion.475), channel_id=1, replica_groups=mesh['rows'=64,'rhs'=8] {'rows'}, use_global_device_ids=true, to_apply=%region_35.39 | all-reduce | flops 1024 | bytes 8192 | tf_op jit(solution)/shard_map/psum | solution.py:115
  523.9 24.5 %all_gather.19 = f32[64,64]{0,1:T(8,128)S(1)} all-gather(f32[64,8]{0,1:T(8,128)S(1)} %get-tuple-element.5610), channel_id=1, replica_groups=mesh['rows'=64,'rhs'=8] {'rhs'}, dimensions={1}, use_global_device_ids=true | all-gather | bytes 18432 | tf_op jit(solution)/shard_map/all_gather | solution.py:116
  561.3 16.7 %while.496 = (s32[]{:T(128)}, f32[8,16,64]{2,0,1:T(8,128)S(1)}, f32[8,8,64]{2,0,1:T(8,128)S(1)}, s32[8,7]{1,0:T(8,128)S(1)}, f32[8,7,64,64]{3,2,1,0:T(8,128)}, /...) while((s32[]{:T(128)}, f32[8,16,64]{2,0,1:T(8,128)S(1)}, ...), condition=%wide.region_37.43_spmd, body=%wide.region_36.42_spmd.sunk | while | flops 3150896 | bytes 322845 | solution.py:71
  586.6 16.7 %while.497 = (s32[]{:T(128)}, f32[8,16,64]{2,0,1:T(8,128)S(1)}, f32[8,8,64]{2,0,1:T(8,128)S(1)}, s32[8,7]{1,0:T(8,128)S(1)}, f32[8,7,64,64]{3,2,1,0:T(8,128)}, /...) while((s32[]{:T(128)}, f32[8,16,64]{2,0,1:T(8,128)S(1)}, ...), condition=%wide.region_39.45_spmd, body=%wide.region_38.44_spmd.sunk | while | flops 3150896 | bytes 322845 | solution.py:71
  605.3 6.6 collective-permute-done.17
  611.9 16.7 %while.498 = (s32[]{:T(128)}, f32[8,16,64]{2,0,1:T(8,128)S(1)}, f32[8,8,64]{2,0,1:T(8,128)S(1)}, s32[8,7]{1,0:T(8,128)S(1)}, f32[8,7,64,64]{3,2,1,0:T(8,128)}, /...) while((s32[]{:T(128)}, f32[8,16,64]{2,0,1:T(8,128)S(1)}, ...), condition=%wide.region_41.47_spmd, body=%wide.region_40.46_spmd.sunk | while | flops 3150896 | bytes 322845 | solution.py:71
  630.6 6.6 collective-permute-done.18
  637.2 16.7 %while.499 = (s32[]{:T(128)}, f32[8,16,64]{2,0,1:T(8,128)S(1)}, f32[8,8,64]{2,0,1:T(8,128)S(1)}, s32[8,7]{1,0:T(8,128)S(1)}, f32[8,7,64,64]{3,2,1,0:T(8,128)}, /...) while((s32[]{:T(128)}, f32[8,16,64]{2,0,1:T(8,128)S(1)}, ...), condition=%wide.region_43.49_spmd, body=%wide.region_42.48_spmd.sunk | while | flops 3150896 | bytes 322845 | solution.py:71
  662.5 16.7 %while.500 = (s32[]{:T(128)}, f32[8,16,64]{2,0,1:T(8,128)S(1)}, f32[8,8,64]{2,0,1:T(8,128)S(1)}, s32[8,7]{1,0:T(8,128)S(1)}, f32[8,7,64,64]{3,2,1,0:T(8,128)}, /...) while((s32[]{:T(128)}, f32[8,16,64]{2,0,1:T(8,128)S(1)}, ...), condition=%wide.region_45.51_spmd, body=%wide.region_44.50_spmd.sunk | while | flops 3150896 | bytes 322845 | solution.py:71
  687.8 16.7 %while.501 = (s32[]{:T(128)}, f32[8,16,64]{2,0,1:T(8,128)S(1)}, f32[8,8,64]{2,0,1:T(8,128)S(1)}, s32[8,7]{1,0:T(8,128)S(1)}, f32[8,7,64,64]{3,2,1,0:T(8,128)}, /...) while((s32[]{:T(128)}, f32[8,16,64]{2,0,1:T(8,128)S(1)}, ...), condition=%wide.region_47.53_spmd, body=%wide.region_46.52_spmd.sunk | while | flops 3150896 | bytes 322845 | solution.py:71
  706.5 6.6 collective-permute-done.21
  713.1 16.7 %while.502 = (s32[]{:T(128)}, f32[8,16,64]{2,0,1:T(8,128)S(1)}, f32[8,8,64]{2,0,1:T(8,128)S(1)}, s32[8,7]{1,0:T(8,128)S(1)}, f32[8,7,64,64]{3,2,1,0:T(8,128)}, /...) while((s32[]{:T(128)}, f32[8,16,64]{2,0,1:T(8,128)S(1)}, ...), condition=%wide.region_49.55_spmd, body=%wide.region_48.54_spmd.sunk | while | flops 3150896 | bytes 322845 | solution.py:71
  738.4 16.7 %while.503 = (s32[]{:T(128)}, f32[8,16,64]{2,0,1:T(8,128)S(1)}, f32[8,8,64]{2,0,1:T(8,128)S(1)}, s32[8,7]{1,0:T(8,128)S(1)}, f32[8,7,64,64]{3,2,1,0:T(8,128)}, /...) while((s32[]{:T(128)}, f32[8,16,64]{2,0,1:T(8,128)S(1)}, ...), condition=%wide.region_51.57_spmd, body=%wide.region_50.56_spmd.sunk | while | flops 3150896 | bytes 322845 | solution.py:71
  755.2 9.2 while.504
  767.9 9.2 while.505
  777.1 7.0 collective-permute-start.24
  785.7 9.2 while.506
  794.9 7.0 collective-permute-start.25
  803.5 9.2 while.507
  812.7 7.0 collective-permute-start.26
  821.3 9.2 while.508
  830.5 7.0 collective-permute-start.27
  839.1 9.2 while.509
  848.3 7.0 collective-permute-start.28
  856.9 9.2 while.510
  866.1 7.0 collective-permute-start.29
  874.7 9.2 while.511
  884.2 129.3 %psum.37 = f32[64,8]{0,1:T(8,128)S(1)} all-reduce(f32[64,8]{0,1:T(8,128)S(1)} %fusion.478), channel_id=1, replica_groups=mesh['rows'=64,'rhs'=8] {'rows'}, use_global_device_ids=true, to_apply=%region_68.74 | all-reduce | flops 512 | bytes 4096 | tf_op jit(solution)/shard_map/psum | solution.py:125
  1015.9 7.0 collective-permute-start.31
  1022.8 24.6 %all_gather.21 = f32[64,512]{1,0:T(8,128)S(1)} all-gather(f32[8,512]{1,0:T(8,128)S(1)} %convolution_add_fusion.1), channel_id=1, replica_groups=mesh['rows'=64,'rhs'=8] {'rhs'}, dimensions={0}, use_global_device_ids=true | all-gather | bytes 147456 | tf_op jit(solution)/shard_map/all_gather | solution.py:112
  1050.5 24.6 %all_gather.23 = f32[64,512]{1,0:T(8,128)S(1)} all-gather(f32[8,512]{1,0:T(8,128)S(1)} %reshape.71), channel_id=1, replica_groups=mesh['rows'=64,'rhs'=8] {'rhs'}, dimensions={0}, use_global_device_ids=true | all-gather | bytes 147456 | tf_op jit(solution)/shard_map/all_gather | solution.py:131
  1075.2 126.1 %all-reduce.28 = (f32[64,8]{0,1:T(8,128)S(1)}, f32[64,8]{0,1:T(8,128)S(1)}) all-reduce(f32[64,8]{0,1:T(8,128)S(1)} %fusion.480, f32[64,8]{0,1:T(8,128)S(1)} %fusion.479), channel_id=1, replica_groups=mesh['rows'=64,'rhs'=8] {'rows'}, use_global_device_ids=true, to_apply=%region_70.76 | all-reduce | flops 1024 | bytes 8192 | tf_op jit(solution)/shard_map/psum | solution.py:115
  1201.3 24.5 %all_gather.22 = f32[64,64]{0,1:T(8,128)S(1)} all-gather(f32[64,8]{0,1:T(8,128)S(1)} %get-tuple-element.5608), channel_id=1, replica_groups=mesh['rows'=64,'rhs'=8] {'rhs'}, dimensions={1}, use_global_device_ids=true | all-gather | bytes 18432 | tf_op jit(solution)/shard_map/all_gather | solution.py:116
  (1483 shorter events, 539.3 us)
Async XLA Ops:
  2.9 3.1 copy-start
  22.7 8.6 collective-permute-start
  48.0 8.6 collective-permute-start.1
  73.3 8.6 collective-permute-start.2
  98.6 8.6 collective-permute-start.3
  123.9 8.6 collective-permute-start.4
  149.2 8.6 collective-permute-start.5
  174.5 8.6 collective-permute-start.6
  209.1 3.5 collective-permute-start.7
  221.8 8.6 collective-permute-start.8
  239.6 8.6 collective-permute-start.9
  257.4 8.6 collective-permute-start.10
  275.2 8.6 collective-permute-start.11
  293.0 8.6 collective-permute-start.12
  310.8 57.8 %copy-start.2 = (f32[8,512]{1,0:T(8,128)S(1)}, f32[8,512]{1,0:T(8,128)}, u32[]{:S(2)}) copy-start(f32[8,512]{1,0:T(8,128)} %param.77) | copy-start | bytes 49156
  310.8 8.6 collective-permute-start.13
  328.7 40.0 %collective-permute-start.14 = (f32[8,512]{1,0:T(8,128)S(1)}, f32[8,512]{1,0:T(8,128)S(1)}, u32[]{:S(2)}, u32[]{:S(2)}) collective-permute-start(f32[8,512]{1,0:T(8,128)S(1)} %reshape.66), channel_id=1, source_target_pairs={{0,8},{8,16},{16,24},{24,32},{32,40},{40,48},{48,56},{56,64},{64,7... | collective-permute-start | bytes 49160 | tf_op jit(solution)/shard_map/ppermute | solution.py:21
  330.6 38.2 %collective-permute-start.15 = (f32[8,512]{1,0:T(8,128)S(1)}, f32[8,512]{1,0:T(8,128)S(1)}, u32[]{:S(2)}, u32[]{:S(2)}) collective-permute-start(f32[8,512]{1,0:T(8,128)S(1)} %reshape.66), channel_id=1, source_target_pairs={{8,0},{16,8},{24,16},{32,24},{40,32},{48,40},{56,48},{64,56},{72,6... | collective-permute-start | bytes 49160 | tf_op jit(solution)/shard_map/ppermute | solution.py:24
  578.0 8.6 collective-permute-start.16
  603.3 8.6 collective-permute-start.17
  628.6 8.6 collective-permute-start.18
  653.9 8.6 collective-permute-start.19
  679.2 8.6 collective-permute-start.20
  704.5 8.6 collective-permute-start.21
  729.8 8.6 collective-permute-start.22
  764.4 3.5 collective-permute-start.23
  777.1 8.6 collective-permute-start.24
  794.9 8.6 collective-permute-start.25
  812.7 8.6 collective-permute-start.26
  830.5 8.6 collective-permute-start.27
  848.3 8.6 collective-permute-start.28
  866.1 8.6 collective-permute-start.29
  883.9 164.5 %copy-start.1 = (f32[8,7,64,64]{3,2,1,0:T(8,128)S(1)}, f32[8,7,64,64]{3,2,1,0:T(8,128)}, u32[]{:S(2)}) copy-start(f32[8,7,64,64]{3,2,1,0:T(8,128)} %param.78) | copy-start | bytes 2752516
  1013.9 33.6 %collective-permute-start.30 = (f32[8,512]{1,0:T(8,128)S(1)}, f32[8,512]{1,0:T(8,128)S(1)}, u32[]{:S(2)}, u32[]{:S(2)}) collective-permute-start(f32[8,512]{1,0:T(8,128)S(1)} %convolution_add_fusion.1), channel_id=1, source_target_pairs={{0,8},{8,16},{16,24},{24,32},{32,40},{40,48},{48,56},{56,64},{64,7... | collective-permute-start | bytes 49160 | tf_op jit(solution)/shard_map/ppermute | solution.py:21
  1015.9 31.8 %collective-permute-start.31 = (f32[8,512]{1,0:T(8,128)S(1)}, f32[8,512]{1,0:T(8,128)S(1)}, u32[]{:S(2)}, u32[]{:S(2)}) collective-permute-start(f32[8,512]{1,0:T(8,128)S(1)} %convolution_add_fusion.1), channel_id=1, source_target_pairs={{8,0},{16,8},{24,16},{32,24},{40,32},{48,40},{56,48},{64,56},{72,6... | collective-permute-start | bytes 49160 | tf_op jit(solution)/shard_map/ppermute | solution.py:24
where the time goes:
time: 1240 us
  blocking collectives  535 us (43%)
  matrix products  265 us (21%)
  local copies, waits for them, and re-layouts  146 us (12%)
  starting transfers between devices  133 us (11%)
  waiting for transfers between devices  114 us (9%)
  other arithmetic  39.3 us (3%)
    psum x2, blocking collectives, shards(): summed_pq, summed_pr = lax.psum((partial_pq, partial_pr), 'rows')  252 us
    dot_general x128, matrix products, forward_one_row(): jnp.einsum('kab,ckb->ca', lower_tiles[row], picked, precision=lax.Precisi...  162 us
    psum x1, blocking collectives, shards(): summed_qz = lax.psum(inner(every_image, preconditioned), 'rows')  129 us
    ppermute x28, starting transfers between devices, passed_along(): lax.ppermute(value, axis, [(source, source + steps) for source in range(f...  115 us
    ppermute x28, waiting for transfers between devices, passed_along(): lax.ppermute(value, axis, [(source, source + steps) for source in range(f...  114 us
    gather x128, local copies, waits for them, and re-layouts, forward_one_row(): picked = jnp.take(extended, forward_cols[row], axis=1)  70.9 us
    gather x128, local copies, waits for them, and re-layouts, backward_one_row(): picked = jnp.take(extended, backward_cols[row], axis=1)  70.9 us
    all_gather x2, blocking collectives, shards(): every_direction = lax.all_gather(direction, 'rhs', axis=0, tiled=True)  55.5 us
  transfers between devices with their start and end apart: 32, of which 28 were waited for; matrix products, arithmetic and copies ran while one was open for 0% of the time, Pallas kernels for 0%

commit v1 on v0

--- a/solution.py
+++ b/solution.py
@@ -109,7 +109,9 @@
         image = jnp.einsum(
             "ikab,cikb->cia", tiles, apply_picked, precision=lax.Precision.HIGHEST
         ).reshape(count, cells)
-        every_direction = lax.all_gather(direction, "rhs", axis=0, tiled=True)
+        every_direction = jnp.concatenate(
+            lax.all_to_all(jnp.stack([direction] * lax.axis_size("rhs")), "rhs", 0, 0), axis=0
+        )
         partial_pq = inner(every_direction, image)
         partial_pr = inner(every_direction, residual)
         summed_pq, summed_pr = lax.psum((partial_pq, partial_pr), "rows")

time: 1240 us -> 1210 us (0.976)
  blocking collectives: 535 us -> 483 us
  starting transfers between devices: 133 us -> 149 us
    all_gather x2 -> x0, blocking collectives: 55.5 us -> none  [shards(): every_direction = lax.all_gather(direction, 'rhs', axis=0, tiled=True)]
    all_to_all x0 -> x2, starting transfers between devices: none -> 16.2 us  [shards(): lax.all_to_all(jnp.stack([direction] * lax.axis_size('rhs')), 'rhs', 0, 0)]
  transfers between devices with their start and end apart: 32 -> 34, of which waited for: 28 -> 28; matrix products, arithmetic and copies ran while one was open for 0% -> 1% of each run, Pallas kernels for 0% -> 0%
where the time goes in v1:
time: 1210 us
  blocking collectives  483 us (40%)
  matrix products  265 us (22%)
  starting transfers between devices  149 us (12%)
  local copies, waits for them, and re-layouts  147 us (12%)
  waiting for transfers between devices  115 us (10%)
  other arithmetic  39.2 us (3%)
    psum x2, blocking collectives, shards(): summed_pq, summed_pr = lax.psum((partial_pq, partial_pr), 'rows')  252 us
    dot_general x128, matrix products, forward_one_row(): jnp.einsum('kab,ckb->ca', lower_tiles[row], picked, precision=lax.Precisi...  162 us
    psum x1, blocking collectives, shards(): summed_qz = lax.psum(inner(every_image, preconditioned), 'rows')  129 us
    ppermute x28, starting transfers between devices, passed_along(): lax.ppermute(value, axis, [(source, source + steps) for source in range(f...  115 us
    ppermute x28, waiting for transfers between devices, passed_along(): lax.ppermute(value, axis, [(source, source + steps) for source in range(f...  115 us
    gather x128, local copies, waits for them, and re-layouts, forward_one_row(): picked = jnp.take(extended, forward_cols[row], axis=1)  70.9 us
    gather x128, local copies, waits for them, and re-layouts, backward_one_row(): picked = jnp.take(extended, backward_cols[row], axis=1)  70.9 us
    all_gather x2, blocking collectives, shards(): every_image = lax.all_gather(image, 'rhs', axis=0, tiled=True)  52.1 us
  transfers between devices with their start and end apart: 34, of which 28 were waited for; matrix products, arithmetic and copies ran while one was open for 1% of the time, Pallas kernels for 0%

profile of v1, /device:TPU:32, one launch (start us, length us, event | category | flops | bytes accessed | tf_op | source)
XLA Modules:
  0.0 1205.0 jit_solution(1830713024037099838)
XLA Ops:
  6.0 16.7 %while.480 = (s32[]{:T(128)}, f32[8,16,64]{2,0,1:T(8,128)S(1)}, f32[8,8,64]{2,0,1:T(8,128)S(1)}, s32[8,7]{1,0:T(8,128)S(1)}, f32[8,7,64,64]{3,2,1,0:T(8,128)}, /...) while((s32[]{:T(128)}, f32[8,16,64]{2,0,1:T(8,128)S(1)}, ...), condition=%wide.region_1.3_spmd, body=%wide.region_0.2_spmd.sunk | while | flops 3150896 | bytes 322845 | solution.py:71
  31.3 16.7 %while.481 = (s32[]{:T(128)}, f32[8,16,64]{2,0,1:T(8,128)S(1)}, f32[8,8,64]{2,0,1:T(8,128)S(1)}, s32[8,7]{1,0:T(8,128)S(1)}, f32[8,7,64,64]{3,2,1,0:T(8,128)}, /...) while((s32[]{:T(128)}, f32[8,16,64]{2,0,1:T(8,128)S(1)}, ...), condition=%wide.region_3.5_spmd, body=%wide.region_2.4_spmd.sunk | while | flops 3150896 | bytes 322845 | solution.py:71
  50.0 6.6 collective-permute-done.1
  56.6 16.7 %while.482 = (s32[]{:T(128)}, f32[8,16,64]{2,0,1:T(8,128)S(1)}, f32[8,8,64]{2,0,1:T(8,128)S(1)}, s32[8,7]{1,0:T(8,128)S(1)}, f32[8,7,64,64]{3,2,1,0:T(8,128)}, /...) while((s32[]{:T(128)}, f32[8,16,64]{2,0,1:T(8,128)S(1)}, ...), condition=%wide.region_5.7_spmd, body=%wide.region_4.6_spmd.sunk | while | flops 3150896 | bytes 322845 | solution.py:71
  75.3 6.6 collective-permute-done.2
  81.9 16.7 %while.483 = (s32[]{:T(128)}, f32[8,16,64]{2,0,1:T(8,128)S(1)}, f32[8,8,64]{2,0,1:T(8,128)S(1)}, s32[8,7]{1,0:T(8,128)S(1)}, f32[8,7,64,64]{3,2,1,0:T(8,128)}, /...) while((s32[]{:T(128)}, f32[8,16,64]{2,0,1:T(8,128)S(1)}, ...), condition=%wide.region_7.9_spmd, body=%wide.region_6.8_spmd.sunk | while | flops 3150896 | bytes 322845 | solution.py:71
  100.6 6.6 collective-permute-done.3
  107.2 16.7 %while.484 = (s32[]{:T(128)}, f32[8,16,64]{2,0,1:T(8,128)S(1)}, f32[8,8,64]{2,0,1:T(8,128)S(1)}, s32[8,7]{1,0:T(8,128)S(1)}, f32[8,7,64,64]{3,2,1,0:T(8,128)}, /...) while((s32[]{:T(128)}, f32[8,16,64]{2,0,1:T(8,128)S(1)}, ...), condition=%wide.region_9.11_spmd, body=%wide.region_8.10_spmd.sunk | while | flops 3150896 | bytes 322845 | solution.py:71
  125.9 6.6 collective-permute-done.4
  132.5 16.7 %while.485 = (s32[]{:T(128)}, f32[8,16,64]{2,0,1:T(8,128)S(1)}, f32[8,8,64]{2,0,1:T(8,128)S(1)}, s32[8,7]{1,0:T(8,128)S(1)}, f32[8,7,64,64]{3,2,1,0:T(8,128)}, /...) while((s32[]{:T(128)}, f32[8,16,64]{2,0,1:T(8,128)S(1)}, ...), condition=%wide.region_11.13_spmd, body=%wide.region_10.12_spmd.sunk | while | flops 3150896 | bytes 322845 | solution.py:71
  151.2 6.6 collective-permute-done.5
  157.8 16.7 %while.486 = (s32[]{:T(128)}, f32[8,16,64]{2,0,1:T(8,128)S(1)}, f32[8,8,64]{2,0,1:T(8,128)S(1)}, s32[8,7]{1,0:T(8,128)S(1)}, f32[8,7,64,64]{3,2,1,0:T(8,128)}, /...) while((s32[]{:T(128)}, f32[8,16,64]{2,0,1:T(8,128)S(1)}, ...), condition=%wide.region_13.15_spmd, body=%wide.region_12.14_spmd.sunk | while | flops 3150896 | bytes 322845 | solution.py:71
  176.5 6.6 collective-permute-done.6
  183.1 16.7 %while.487 = (s32[]{:T(128)}, f32[8,16,64]{2,0,1:T(8,128)S(1)}, f32[8,8,64]{2,0,1:T(8,128)S(1)}, s32[8,7]{1,0:T(8,128)S(1)}, f32[8,7,64,64]{3,2,1,0:T(8,128)}, /...) while((s32[]{:T(128)}, f32[8,16,64]{2,0,1:T(8,128)S(1)}, ...), condition=%wide.region_15.17_spmd, body=%wide.region_14.16_spmd.sunk | while | flops 3150896 | bytes 322845 | solution.py:71
  199.9 9.2 while.488
  212.6 9.2 while.489
  221.8 7.0 collective-permute-start.8
  230.4 9.2 while.490
  239.6 7.0 collective-permute-start.9
  248.2 9.2 while.491
  257.4 7.0 collective-permute-start.10
  266.0 9.2 while.492
  275.2 7.0 collective-permute-start.11
  283.8 9.2 while.493
  293.0 7.0 collective-permute-start.12
  301.6 9.2 while.494
  310.8 7.0 collective-permute-start.13
  319.4 9.2 while.495
  330.6 7.0 collective-permute-start.15
  338.3 10.4 all-to-all-start
  353.0 26.0 %all_gather.13 = f32[64,512]{1,0:T(8,128)S(1)} all-gather(f32[8,512]{1,0:T(8,128)S(1)} %reshape.75), channel_id=1, replica_groups=mesh['rows'=64,'rhs'=8] {'rhs'}, dimensions={0}, use_global_device_ids=true | all-gather | bytes 147456 | tf_op jit(solution)/shard_map/all_gather | solution.py:124
  379.4 126.1 %all-reduce.29 = (f32[64,8]{0,1:T(8,128)S(1)}, f32[64,8]{0,1:T(8,128)S(1)}) all-reduce(f32[64,8]{0,1:T(8,128)S(1)} %fusion.460, f32[64,8]{0,1:T(8,128)S(1)} %fusion.462), channel_id=1, replica_groups=mesh['rows'=64,'rhs'=8] {'rows'}, use_global_device_ids=true, to_apply=%region_35.39 | all-reduce | flops 1024 | bytes 8192 | tf_op jit(solution)/shard_map/psum | solution.py:117
  505.6 24.5 %all_gather.12 = f32[64,64]{0,1:T(8,128)S(1)} all-gather(f32[64,8]{0,1:T(8,128)S(1)} %get-tuple-element.5610), channel_id=1, replica_groups=mesh['rows'=64,'rhs'=8] {'rhs'}, dimensions={1}, use_global_device_ids=true | all-gather | bytes 18432 | tf_op jit(solution)/shard_map/all_gather | solution.py:118
  543.0 16.7 %while.496 = (s32[]{:T(128)}, f32[8,16,64]{2,0,1:T(8,128)S(1)}, f32[8,8,64]{2,0,1:T(8,128)S(1)}, s32[8,7]{1,0:T(8,128)S(1)}, f32[8,7,64,64]{3,2,1,0:T(8,128)}, /...) while((s32[]{:T(128)}, f32[8,16,64]{2,0,1:T(8,128)S(1)}, ...), condition=%wide.region_37.43_spmd, body=%wide.region_36.42_spmd.sunk | while | flops 3150896 | bytes 322845 | solution.py:71
  568.3 16.7 %while.497 = (s32[]{:T(128)}, f32[8,16,64]{2,0,1:T(8,128)S(1)}, f32[8,8,64]{2,0,1:T(8,128)S(1)}, s32[8,7]{1,0:T(8,128)S(1)}, f32[8,7,64,64]{3,2,1,0:T(8,128)}, /...) while((s32[]{:T(128)}, f32[8,16,64]{2,0,1:T(8,128)S(1)}, ...), condition=%wide.region_39.45_spmd, body=%wide.region_38.44_spmd.sunk | while | flops 3150896 | bytes 322845 | solution.py:71
  586.9 6.6 collective-permute-done.17
  593.6 16.7 %while.498 = (s32[]{:T(128)}, f32[8,16,64]{2,0,1:T(8,128)S(1)}, f32[8,8,64]{2,0,1:T(8,128)S(1)}, s32[8,7]{1,0:T(8,128)S(1)}, f32[8,7,64,64]{3,2,1,0:T(8,128)}, /...) while((s32[]{:T(128)}, f32[8,16,64]{2,0,1:T(8,128)S(1)}, ...), condition=%wide.region_41.47_spmd, body=%wide.region_40.46_spmd.sunk | while | flops 3150896 | bytes 322845 | solution.py:71
  612.2 6.6 collective-permute-done.18
  618.9 16.7 %while.499 = (s32[]{:T(128)}, f32[8,16,64]{2,0,1:T(8,128)S(1)}, f32[8,8,64]{2,0,1:T(8,128)S(1)}, s32[8,7]{1,0:T(8,128)S(1)}, f32[8,7,64,64]{3,2,1,0:T(8,128)}, /...) while((s32[]{:T(128)}, f32[8,16,64]{2,0,1:T(8,128)S(1)}, ...), condition=%wide.region_43.49_spmd, body=%wide.region_42.48_spmd.sunk | while | flops 3150896 | bytes 322845 | solution.py:71
  637.5 6.6 collective-permute-done.19
  644.2 16.7 %while.500 = (s32[]{:T(128)}, f32[8,16,64]{2,0,1:T(8,128)S(1)}, f32[8,8,64]{2,0,1:T(8,128)S(1)}, s32[8,7]{1,0:T(8,128)S(1)}, f32[8,7,64,64]{3,2,1,0:T(8,128)}, /...) while((s32[]{:T(128)}, f32[8,16,64]{2,0,1:T(8,128)S(1)}, ...), condition=%wide.region_45.51_spmd, body=%wide.region_44.50_spmd.sunk | while | flops 3150896 | bytes 322845 | solution.py:71
  662.8 6.6 collective-permute-done.20
  669.5 16.7 %while.501 = (s32[]{:T(128)}, f32[8,16,64]{2,0,1:T(8,128)S(1)}, f32[8,8,64]{2,0,1:T(8,128)S(1)}, s32[8,7]{1,0:T(8,128)S(1)}, f32[8,7,64,64]{3,2,1,0:T(8,128)}, /...) while((s32[]{:T(128)}, f32[8,16,64]{2,0,1:T(8,128)S(1)}, ...), condition=%wide.region_47.53_spmd, body=%wide.region_46.52_spmd.sunk | while | flops 3150896 | bytes 322845 | solution.py:71
  694.8 16.7 %while.502 = (s32[]{:T(128)}, f32[8,16,64]{2,0,1:T(8,128)S(1)}, f32[8,8,64]{2,0,1:T(8,128)S(1)}, s32[8,7]{1,0:T(8,128)S(1)}, f32[8,7,64,64]{3,2,1,0:T(8,128)}, /...) while((s32[]{:T(128)}, f32[8,16,64]{2,0,1:T(8,128)S(1)}, ...), condition=%wide.region_49.55_spmd, body=%wide.region_48.54_spmd.sunk | while | flops 3150896 | bytes 322845 | solution.py:71
  720.1 16.7 %while.503 = (s32[]{:T(128)}, f32[8,16,64]{2,0,1:T(8,128)S(1)}, f32[8,8,64]{2,0,1:T(8,128)S(1)}, s32[8,7]{1,0:T(8,128)S(1)}, f32[8,7,64,64]{3,2,1,0:T(8,128)}, /...) while((s32[]{:T(128)}, f32[8,16,64]{2,0,1:T(8,128)S(1)}, ...), condition=%wide.region_51.57_spmd, body=%wide.region_50.56_spmd.sunk | while | flops 3150896 | bytes 322845 | solution.py:71
  736.8 9.2 while.504
  749.6 9.2 while.505
  758.8 7.0 collective-permute-start.24
  767.4 9.2 while.506
  776.6 7.0 collective-permute-start.25
  785.2 9.2 while.507
  794.4 7.0 collective-permute-start.26
  802.9 9.2 while.508
  812.2 7.0 collective-permute-start.27
  820.7 9.2 while.509
  830.0 7.0 collective-permute-start.28
  838.5 9.2 while.510
  847.7 7.0 collective-permute-start.29
  856.3 9.2 while.511
  865.8 129.3 %psum.37 = f32[64,8]{0,1:T(8,128)S(1)} all-reduce(f32[64,8]{0,1:T(8,128)S(1)} %fusion.487), channel_id=1, replica_groups=mesh['rows'=64,'rhs'=8] {'rows'}, use_global_device_ids=true, to_apply=%region_68.74 | all-reduce | flops 512 | bytes 4096 | tf_op jit(solution)/shard_map/psum | solution.py:127
  997.5 7.0 collective-permute-start.31
  1013.8 26.0 %all_gather.15 = f32[64,512]{1,0:T(8,128)S(1)} all-gather(f32[8,512]{1,0:T(8,128)S(1)} %reshape.80), channel_id=1, replica_groups=mesh['rows'=64,'rhs'=8] {'rhs'}, dimensions={0}, use_global_device_ids=true | all-gather | bytes 147456 | tf_op jit(solution)/shard_map/all_gather | solution.py:133
  1040.2 126.1 %all-reduce.28 = (f32[64,8]{0,1:T(8,128)S(1)}, f32[64,8]{0,1:T(8,128)S(1)}) all-reduce(f32[64,8]{0,1:T(8,128)S(1)} %fusion.453, f32[64,8]{0,1:T(8,128)S(1)} %fusion.455), channel_id=1, replica_groups=mesh['rows'=64,'rhs'=8] {'rows'}, use_global_device_ids=true, to_apply=%region_70.76 | all-reduce | flops 1024 | bytes 8192 | tf_op jit(solution)/shard_map/psum | solution.py:117
  1166.4 24.5 %all_gather.14 = f32[64,64]{0,1:T(8,128)S(1)} all-gather(f32[64,8]{0,1:T(8,128)S(1)} %get-tuple-element.5608), channel_id=1, replica_groups=mesh['rows'=64,'rhs'=8] {'rhs'}, dimensions={1}, use_global_device_ids=true | all-gather | bytes 18432 | tf_op jit(solution)/shard_map/all_gather | solution.py:118
  (1487 shorter events, 539.9 us)
Async XLA Ops:
  2.9 3.1 copy-start
  22.7 8.6 collective-permute-start
  48.0 8.6 collective-permute-start.1
  73.3 8.6 collective-permute-start.2
  98.6 8.6 collective-permute-start.3
  123.9 8.6 collective-permute-start.4
  149.2 8.6 collective-permute-start.5
  174.5 8.6 collective-permute-start.6
  209.1 3.5 collective-permute-start.7
  221.8 8.6 collective-permute-start.8
  239.6 8.6 collective-permute-start.9
  257.4 8.6 collective-permute-start.10
  275.2 8.6 collective-permute-start.11
  293.0 8.6 collective-permute-start.12
  310.8 8.6 collective-permute-start.13
  328.7 20.0 %collective-permute-start.14 = (f32[8,512]{1,0:T(8,128)S(1)}, f32[8,512]{1,0:T(8,128)S(1)}, u32[]{:S(2)}, u32[]{:S(2)}) collective-permute-start(f32[8,512]{1,0:T(8,128)S(1)} %stack_reshape.2), channel_id=1, source_target_pairs={{0,8},{8,16},{16,24},{24,32},{32,40},{40,48},{48,56},{56,64},{64,7... | collective-permute-start | bytes 49160 | tf_op jit(solution)/shard_map/ppermute | solution.py:21
  330.6 18.2 %collective-permute-start.15 = (f32[8,512]{1,0:T(8,128)S(1)}, f32[8,512]{1,0:T(8,128)S(1)}, u32[]{:S(2)}, u32[]{:S(2)}) collective-permute-start(f32[8,512]{1,0:T(8,128)S(1)} %stack_reshape.2), channel_id=1, source_target_pairs={{8,0},{16,8},{24,16},{32,24},{40,32},{48,40},{56,48},{64,56},{72,6... | collective-permute-start | bytes 49160 | tf_op jit(solution)/shard_map/ppermute | solution.py:24
  338.3 41.0 %copy-start.2 = (f32[8,512]{1,0:T(8,128)S(1)}, f32[8,512]{1,0:T(8,128)}, u32[]{:S(2)}) copy-start(f32[8,512]{1,0:T(8,128)} %param.77) | copy-start | bytes 49156
  338.3 40.8 %all-to-all-start = ((f32[8,8,512]{2,1,0:T(8,128)}), f32[8,8,512]{2,1,0:T(8,128)S(1)}, u32[]{:S(2)}, u32[]{:S(2)}) async-start(f32[8,8,512]{2,1,0:T(8,128)} %stack.4), calls=%async_computation | async-start | bytes 262144 | tf_op jit(solution)/shard_map/all_to_all | solution.py:113
  559.7 8.6 collective-permute-start.16
  585.0 8.6 collective-permute-start.17
  610.3 8.6 collective-permute-start.18
  635.6 8.6 collective-permute-start.19
  660.9 8.6 collective-permute-start.20
  686.2 8.6 collective-permute-start.21
  711.5 8.6 collective-permute-start.22
  746.0 3.5 collective-permute-start.23
  758.8 8.6 collective-permute-start.24
  776.6 8.6 collective-permute-start.25
  794.4 8.6 collective-permute-start.26
  812.2 8.6 collective-permute-start.27
  830.0 8.6 collective-permute-start.28
  847.7 8.6 collective-permute-start.29
  865.5 146.3 %copy-start.1 = (f32[8,7,64,64]{3,2,1,0:T(8,128)S(1)}, f32[8,7,64,64]{3,2,1,0:T(8,128)}, u32[]{:S(2)}) copy-start(f32[8,7,64,64]{3,2,1,0:T(8,128)} %param.78) | copy-start | bytes 2752516
  995.6 15.5 %collective-permute-start.30 = (f32[8,512]{1,0:T(8,128)S(1)}, f32[8,512]{1,0:T(8,128)S(1)}, u32[]{:S(2)}, u32[]{:S(2)}) collective-permute-start(f32[8,512]{1,0:T(8,128)S(1)} %convolution_add_fusion.1), channel_id=1, source_target_pairs={{0,8},{8,16},{16,24},{24,32},{32,40},{40,48},{48,56},{56,64},{64,7... | collective-permute-start | bytes 49160 | tf_op jit(solution)/shard_map/ppermute | solution.py:21
  997.5 13.6 %collective-permute-start.31 = (f32[8,512]{1,0:T(8,128)S(1)}, f32[8,512]{1,0:T(8,128)S(1)}, u32[]{:S(2)}, u32[]{:S(2)}) collective-permute-start(f32[8,512]{1,0:T(8,128)S(1)} %convolution_add_fusion.1), channel_id=1, source_target_pairs={{8,0},{16,8},{24,16},{32,24},{40,32},{48,40},{56,48},{64,56},{72,6... | collective-permute-start | bytes 49160 | tf_op jit(solution)/shard_map/ppermute | solution.py:24
  1005.3 34.5 %all-to-all-start.1 = ((f32[8,8,512]{2,1,0:T(8,128)}), f32[8,8,512]{2,1,0:T(8,128)S(1)}, u32[]{:S(2)}, u32[]{:S(2)}) async-start(f32[8,8,512]{2,1,0:T(8,128)} %stack.5), calls=%async_computation.1 | async-start | bytes 262144 | tf_op jit(solution)/shard_map/all_to_all | solution.py:113
